TPU v7x, 256 devices: a whole 4x4x8 slice. The times are simulated.
256 devices in a mesh: tile: 64 (over x, z_hi, y), sec: 4 (over z_lo, core).
Axes of the slice: x: 4, y: 4, z: 8 (z_hi: 4, z_lo: 2; z = z_hi * 2 + z_lo), core: 2. Of those that a mesh axis runs over, the one named last changes fastest.
Arguments:
- pixels: bfloat16 [8, 512, 1024, 256], P('sec', 'tile'), may hold values from -6 to 6
- pred_features: bfloat16 [512, 1024, 128], P('tile'), may hold values from -6 to 6
- offsets: int32 [8, 2, 512, 1024], P('sec', None, 'tile'), may hold values from -1 to 1
- valid_mask: int32 [8, 512, 1024], P('sec', 'tile'), may hold values 0 or 1
- base_shift: float32 [2, 512, 1024], P(None, 'tile'), may hold values from -6 to 6
- w_hidden: bfloat16 [256, 512], replicated, may hold values from -0.375 to 0.375
- w_feature: bfloat16 [512, 128], replicated, may hold values from -0.25 to 0.25
- feat_gain: float32 [128], replicated, may hold values from 0.25 to 1.75
Outputs:
- displacement: float32 [8, 2, 512, 1024], P('sec', None, 'tile')
All inputs are finite; a program needn't handle non-finite values. No bound on the sum of `valid_mask` on one device may be relied on, other than what follows from the above.
Results may differ from a plain program's by a relative error of at most 0.0024.
Values may be sent and summed in bfloat16 or wider, within the bound.
A program may use at most 128 MiB of HBM per device.

v0:
```python
import jax
import jax.numpy as jnp
from jax import lax
from jax.sharding import PartitionSpec as P

ITERS = 8


epsilon = 1e-05
step_size = 0.2
stiffness = 0.5


def from_behind(value, axis, steps):
    count = lax.axis_size(axis)
    first, last = (max(0, -steps), min(count, count - steps))
    return lax.ppermute(value, axis, [(source, source + steps) for source in range(first, last)])


def with_halo(cells, sides, width):
    for axis, dim in sides:
        count = lax.axis_size(axis)
        ends = count - 1
        head = lax.slice_in_dim(cells, 0, width, axis=dim)
        tail = lax.slice_in_dim(cells, cells.shape[dim] - width, cells.shape[dim], axis=dim)
        cells = jnp.concatenate(
            [
                lax.ppermute(tail, axis, [(i, (i + 1) % count) for i in range(ends)]),
                cells,
                lax.ppermute(head, axis, [((i + 1) % count, i) for i in range(ends)]),
            ],
            axis=dim,
        )
    return cells


def entering(value, axis, join, neutral):
    place = lax.axis_index(axis)
    gathered = lax.all_gather(
        value.astype(jnp.bfloat16 if value.dtype == jnp.float32 else value.dtype), axis
    )
    state = jnp.zeros_like(value) + jnp.asarray(neutral, value.dtype)

    def one(hop, state):
        return join(state, lax.dynamic_index_in_dim(gathered, hop, 0, False).astype(value.dtype))

    return lax.fori_loop(0, place, one, state)


def encode(section_pixels, w_hidden, w_feature, feat_gain):
    flat = section_pixels.reshape(-1, section_pixels.shape[-1])
    hidden = jax.nn.relu(jnp.dot(flat, w_hidden, preferred_element_type=jnp.float32)).astype(
        jnp.bfloat16
    )
    pre = jnp.dot(hidden, w_feature, preferred_element_type=jnp.float32)
    scale = lax.rsqrt(jnp.mean(pre * pre, axis=-1, keepdims=True) + epsilon)
    result = (pre * scale * feat_gain).astype(jnp.bfloat16)
    return result.reshape(section_pixels.shape[:-1] + (w_feature.shape[1],))


def flow_field(feature, ref_rows, offsets):
    rows = feature.shape[-3]
    cols = feature.shape[-2]
    padding = [(0, 0)] * (ref_rows.ndim - 2) + [(2, 2), (0, 0)]
    padded = jnp.pad(ref_rows, padding)
    own = feature.astype(jnp.float32)
    scores = {}
    for shift_y in range(-2, 3):
        for shift_x in range(-2, 3):
            window = padded[
                ..., 2 + shift_y : 2 + shift_y + rows, 2 + shift_x : 2 + shift_x + cols, :
            ]
            scores[shift_y, shift_x] = (
                jnp.sum(own * window.astype(jnp.float32), axis=-1) / own.shape[-1]
            )
    offset_y = offsets[..., 0, :, :]
    offset_x = offsets[..., 1, :, :]
    total = jnp.ones(offset_y.shape, jnp.float32)
    sum_y = jnp.zeros(offset_y.shape, jnp.float32)
    sum_x = jnp.zeros(offset_y.shape, jnp.float32)
    for near_y in (-1, 0, 1):
        for near_x in (-1, 0, 1):
            picked = jnp.zeros(offset_y.shape, jnp.float32)
            for cand_y in (-1, 0, 1):
                for cand_x in (-1, 0, 1):
                    hit = (offset_y == cand_y) & (offset_x == cand_x)
                    picked = picked + jnp.where(hit, scores[cand_y + near_y, cand_x + near_x], 0.0)
            weight = picked * picked
            total = total + weight
            sum_y = sum_y + weight * near_y
            sum_x = sum_x + weight * near_x
    flow_y = offset_y.astype(jnp.float32) + sum_y / total
    flow_x = offset_x.astype(jnp.float32) + sum_x / total
    return jnp.stack([flow_y, flow_x], axis=-3)


def relax_step(padded, flow, weight):
    center = padded[:, :, 1:-1]
    upper = padded[:, :, :-2]
    lower = padded[:, :, 2:]
    sided = jnp.pad(center, ((0, 0), (0, 0), (0, 0), (1, 1)))
    left_side = sided[..., :-2]
    right_side = sided[..., 2:]
    return center + step_size * (
        upper + lower + left_side + right_side - 4.0 * center + weight * (flow - center)
    )


def add_fields(earlier, later):
    return earlier + later


def grid_rows(rows, depth):
    global_row = (
        lax.axis_index("tile") * rows + jnp.arange(rows + 2 * depth, dtype=jnp.int32) - depth
    )
    return ((global_row >= 0) & (global_row < rows * lax.axis_size("tile"))).astype(jnp.float32)


def shards(pixels, pred_features, offsets, valid_mask, base_shift, w_hidden, w_feature, feat_gain):
    features = encode(pixels, w_hidden, w_feature, feat_gain)
    is_first = lax.axis_index("sec") == 0
    passed = from_behind(features[-1], "sec", 1)
    first_ref = jnp.where(is_first, pred_features, passed)
    ref_stack = jnp.concatenate([first_ref[None], features[:-1]], axis=0)
    extended = with_halo(ref_stack, (("tile", 1),), 2)
    flow = flow_field(features, extended, offsets)
    weight = stiffness * valid_mask.astype(jnp.float32)[:, None]
    field = jnp.zeros(flow.shape, jnp.float32)
    rows = field.shape[2]
    targets = with_halo(
        jnp.concatenate([flow, weight], axis=1).astype(jnp.bfloat16), (("tile", 2),), ITERS
    ).astype(jnp.float32)
    inside = grid_rows(rows, ITERS)
    field = jnp.zeros(
        (field.shape[0], field.shape[1], rows + 2 * ITERS, field.shape[3]), jnp.float32
    )
    for step in range(ITERS):
        start = step + 1
        length = rows + 2 * ITERS - 2 * start
        flow_part = targets[:, :2, start : start + length]
        weight_part = targets[:, 2:, start : start + length]
        field = (
            relax_step(field, flow_part, weight_part)
            * inside[start : start + length][None, None, :, None]
        )
    local_total = jnp.sum(field, axis=0)
    prefix = entering(local_total, "sec", add_fields, jnp.zeros_like(local_total))
    running = base_shift + prefix
    results = []
    for index in range(field.shape[0]):
        running = running + field[index]
        results.append(running)
    return jnp.stack(results, axis=0)


def solution(mesh):
    in_specs = (
        P("sec", "tile", None, None),
        P("tile", None, None),
        P("sec", None, "tile", None),
        P("sec", "tile", None),
        P(None, "tile", None),
        P(),
        P(),
        P(),
    )
    out_specs = P("sec", None, "tile", None)
    return jax.shard_map(shards, mesh=mesh, in_specs=in_specs, out_specs=out_specs, check_vma=False)
```

profile of v0, /device:TPU:39, one launch (start us, length us, event | category | flops | bytes accessed | tf_op | source)
XLA Modules:
  0.0 202.6 jit_solution(11563099136008845339)
XLA Ops:
  0.0 0.0 copy-start
  0.0 0.9 copy-done
  1.0 13.5 %multiply_reduce_fusion.24 = (f32[16384]{0:T(1024)S(1)}, f32[16384,128]{1,0:T(8,128)}) fusion(bf16[512,128]{1,0:T(8,128)(2,1)} %param.16, bf16[16384,256]{1,0:T(8,128)(2,1)} %bitcast.951, bf16[256,512]{1,0:T(8,128)(2,1)S(1)} %copy-done), kind=kOutput, calls=%fused_computation.32 | convolution fusion | flops 6463406080 | bytes 17235968 | tf_op jit(solution)/shard_map/dot_general | solution.py:55
  14.5 0.0 copy-done.11
  14.5 0.0 copy-start.9
  14.5 0.0 copy-start.6
  14.5 5.3 %multiply_convert_fusion = bf16[16384,128]{1,0:T(8,128)(2,1)S(1)} fusion(f32[16384,128]{1,0:T(8,128)} %get-tuple-element.106, f32[128]{0:T(128)S(1)} %copy-done.11, f32[16384]{0:T(1024)S(1)} %add_rsqrt_fusion), kind=kLoop, calls=%fused_computation.31 | loop fusion | flops 6291456 | bytes 12648960 | tf_op jit(solution)/shard_map/convert_element_type | solution.py:57
  19.8 0.0 copy-start.4
  19.8 1.9 copy-done.4
  21.8 1.7 fusion.196
  23.4 1.3 collective-permute-start
  24.7 0.6 slice.390
  25.3 0.6 slice.342
  25.9 0.7 slice.350
  26.6 0.5 slice.358
  27.2 0.6 slice.366
  27.8 0.6 slice.374
  28.4 0.6 slice.382
  29.1 0.6 slice_multiply_fusion.1
  29.7 0.0 copy-done.9
  29.7 0.0 copy-done.6
  29.8 0.6 fusion.197
  30.5 0.0 collective-permute-done
  30.5 2.0 select_bitcast_fusion
  32.4 0.0 slice-start.1
  32.5 0.4 pad_maximum_fusion
  32.8 1.5 fusion.6
  34.3 9.9 %collective-permute-start.2 = (bf16[2,2,1024,128]{3,2,1,0:T(8,128)(2,1)}, bf16[2,2,1024,128]{3,2,1,0:T(8,128)(2,1)S(1)}, u32[]{:S(2)}, u32[]{:S(2)}) collective-permute-start(bf16[2,2,1024,128]{3,2,1,0:T(8,128)(2,1)} %get-tuple-element.92), channel_id=1, source_target_pairs={{4,0},{8,4},{12,8},{16,12},{20,16},{24,20},{28,24},{32,28},{36,32}... | collective-permute-start | bytes 3145736 | tf_op jit(solution)/shard_map/ppermute | solution.py:30
  44.2 2.1 %collective-permute-start.1 = (bf16[2,2,1024,128]{3,2,1,0:T(8,128)(2,1)}, bf16[2,2,1024,128]{3,2,1,0:T(8,128)(2,1)}, u32[]{:S(2)}, u32[]{:S(2)}) collective-permute-start(bf16[2,2,1024,128]{3,2,1,0:T(8,128)(2,1)} %get-tuple-element.91), channel_id=1, source_target_pairs={{0,4},{4,8},{8,12},{12,16},{16,20},{20,24},{24,28},{28,32},{32,36}... | collective-permute-start | bytes 3145736 | tf_op jit(solution)/shard_map/ppermute | solution.py:28
  46.3 0.0 slice-done
  46.3 0.0 slice-done.1
  46.3 5.2 %fusion.1 = f32[16384]{0:T(1024)S(1)} fusion(bf16[2,8,1024,128]{3,2,1,0:T(8,128)(2,1)S(1)} %pad_maximum_fusion, f32[128]{0:T(128)S(1)} %copy-done.11, f32[16384,128]{1,0:T(8,128)S(1)} %bitcast.948, f32[16384]{0:T(1024)S(1)} %add_rsqrt_fusion), kind=kLoop, calls=%fused_computation.6 | loop fusion | flops 14663680 | bytes 12714496 | tf_op jit(solution)/shard_map/reduce_sum | solution.py:74
  51.6 19.8 %collective-permute-done.2 = bf16[2,2,1024,128]{3,2,1,0:T(8,128)(2,1)S(1)} collective-permute-done((bf16[2,2,1024,128]{3,2,1,0:T(8,128)(2,1)}, bf16[2,2,1024,128]{3,2,1,0:T(8,128)(2,1)S(1)}, u32[]{:S(2)}, u32[]{:S(2)}) %collective-permute-start.2) | collective-permute-done | bytes 1048608 | tf_op jit(solution)/shard_map/ppermute | solution.py:30
  71.3 0.0 collective-permute-done.1
  71.4 4.8 %select_maximum_fusion = bf16[2,12,1028,128]{3,2,1,0:T(8,128)(2,1)S(1)} fusion(bf16[2,2,1024,128]{3,2,1,0:T(8,128)(2,1)S(1)} %collective-permute-done.2, bf16[2,2,1024,128]{3,2,1,0:T(8,128)(2,1)} %collective-permute-done.1, bf16[1,8,1024,128]{3,2,1,0:T(8,128)(2,1)} %bitcast.942, bf16[1,8,1024,128]{3,2,1,0:T(8,128)(2,1)S(1)} %select_bitcast_fusion), kind=kLoop, calls=%fused_computation.34 | loop fusion | flops 47370240 | bytes 12607488 | tf_op jit(solution)/shard_map/concatenate | solution.py:26
  76.1 4.6 %maximum_maximum_fusion = (bf16[2,10,1024,128]{3,2,1,0:T(8,128)(2,1)S(1)}, bf16[2,10,1024,128]{3,2,1,0:T(8,128)(2,1)}) fusion(bf16[1,8,1024,128]{3,2,1,0:T(8,128)(2,1)S(1)} %bitcast.945, bf16[1,8,1024,128]{3,2,1,0:T(8,128)(2,1)S(1)} %select_bitcast_fusion, bf16[2,2,1024,128]{3,2,1,0:T(8,128)(2,1)} %collective-permute-done.1, ...), kind=kLoop, calls=%fused_computation.44 | loop fusion | flops 10485760 | bytes 16777216 | tf_op jit(solution)/shard_map/concatenate | solution.py:26
  80.7 16.6 %multiply_reduce_fusion.20 = (f32[2,8,1024]{2,1,0:T(8,128)S(1)}, f32[2,8,1024]{2,1,0:T(8,128)S(1)}, f32[2,8,1024]{2,1,0:T(8,128)S(1)}, f32[2,8,1024]{2,1,0:T(8,1...) fusion(bf16[2,12,1028,128]{3,2,1,0:T(8,128)(2,1)S(1)} %select_maximum_fusion, ...), kind=kLoop, calls=%fused_computation.27 | loop fusion | flops 39747584 | bytes 38141952 | tf_op jit(solution)/shard_map/reduce_sum | solution.py:74
  97.3 43.2 %multiply_reduce_fusion.23 = (f32[2,8,1024]{2,1,0:T(8,128)S(1)}, f32[2,8,1024]{2,1,0:T(8,128)S(1)}, f32[2,8,1024]{2,1,0:T(8,128)S(1)}, f32[2,8,1024]{2,1,0:T(8,1...) fusion(f32[2,8,1024,128]{3,2,1,0:T(8,128)} %get-tuple-element.7, ...), kind=kLoop, calls=%fused_computation.30 | loop fusion | flops 112951296 | bytes 85065728 | tf_op jit(solution)/shard_map/reduce_sum | solution.py:74
  140.5 0.5 fusion.178
  141.1 0.1 fusion.167
  141.2 8.8 %collective-permute-start.4 = (bf16[2,3,8,1024]{3,2,1,0:T(8,128)(2,1)S(1)}, bf16[2,3,8,1024]{3,2,1,0:T(8,128)(2,1)S(1)}, u32[]{:S(2)}, u32[]{:S(2)}) collective-permute-start(bf16[2,3,8,1024]{3,2,1,0:T(8,128)(2,1)S(1)} %pad_maximum_fusion.3), channel_id=1, source_target_pairs={{4,0},{8,4},{12,8},{16,12},{20,16},{24,20},{28,24},{32,28},{36,32}... | collective-permute-start | bytes 294920 | tf_op jit(solution)/shard_map/ppermute | solution.py:30
  150.0 2.1 %collective-permute-start.3 = (bf16[2,3,8,1024]{3,2,1,0:T(8,128)(2,1)S(1)}, bf16[2,3,8,1024]{3,2,1,0:T(8,128)(2,1)S(1)}, u32[]{:S(2)}, u32[]{:S(2)}) collective-permute-start(bf16[2,3,8,1024]{3,2,1,0:T(8,128)(2,1)S(1)} %pad_maximum_fusion.3), channel_id=1, source_target_pairs={{0,4},{4,8},{8,12},{12,16},{16,20},{20,24},{24,28},{28,32},{32,36}... | collective-permute-start | bytes 294920 | tf_op jit(solution)/shard_map/ppermute | solution.py:28
  152.2 0.1 fusion.180
  152.3 0.0 collective-permute-done.4
  152.3 8.2 %collective-permute-done.3 = bf16[2,3,8,1024]{3,2,1,0:T(8,128)(2,1)S(1)} collective-permute-done((bf16[2,3,8,1024]{3,2,1,0:T(8,128)(2,1)S(1)}, bf16[2,3,8,1024]{3,2,1,0:T(8,128)(2,1)S(1)}, u32[]{:S(2)}, u32[]{:S(2)}) %collective-permute-start.3) | collective-permute-done | bytes 98336 | tf_op jit(solution)/shard_map/ppermute | solution.py:28
  160.6 0.0 copy-start.13
  160.8 0.0 copy-start.10
  160.8 0.0 copy-start.20
  160.8 0.0 copy-start.1
  160.8 0.1 fusion.25
  161.0 0.3 fusion.14
  161.3 0.3 fusion.21
  161.7 0.0 copy-done.17
  161.7 0.2 fusion.32
  162.0 0.2 fusion.39
  162.2 0.2 fusion.46
  162.5 0.0 copy-done.14
  162.5 0.2 fusion.53
  162.8 0.0 copy-done.13
  162.8 0.1 fusion.183
  162.9 38.8 %all-gather = bf16[8,8,1024]{2,1,0:T(8,128)(2,1)S(1)} all-gather(bf16[2,8,1024]{2,1,0:T(8,128)(2,1)S(1)} %get-tuple-element.65), channel_id=2, replica_groups=mesh['tile'=64,'sec'=4] {'sec'}, dimensions={0}, use_global_device_ids=true | all-gather | bytes 163840 | tf_op jit(solution)/shard_map/all_gather | solution.py:39
  201.8 0.1 while.10
  201.9 0.0 copy-start.21
  201.9 0.6 copy-done.21
  (60 shorter events, 0.6 us)
Async XLA Ops:
  0.0 1.0 copy-start
  1.0 13.6 %copy-start.11 = (f32[128]{0:T(128)S(1)}, f32[128]{0:T(128)}, u32[]{:S(2)}) copy-start(f32[128]{0:T(128)} %param.17) | copy-start | bytes 1540
  14.5 15.2 %copy-start.9 = (s32[2,8,1024]{2,1,0:T(8,128)S(1)}, s32[2,8,1024]{2,1,0:T(8,128)}, u32[]{:S(2)}) copy-start(s32[2,8,1024]{2,1,0:T(8,128)} %param.13) | copy-start | bytes 196612
  14.5 15.2 %copy-start.6 = (s32[2,2,8,1024]{3,2,1,0:T(8,128)S(1)}, s32[2,2,8,1024]{3,2,1,0:T(8,128)}, u32[]{:S(2)}) copy-start(s32[2,2,8,1024]{3,2,1,0:T(8,128)} %param.12) | copy-start | bytes 393220
  19.8 1.9 copy-start.4
  23.4 7.0 %collective-permute-start = (bf16[8,1024,128]{2,1,0:T(8,128)(2,1)S(1)}, bf16[8,1024,128]{2,1,0:T(8,128)(2,1)}, u32[]{:S(2)}, u32[]{:S(2)}) collective-permute-start(bf16[8,1024,128]{2,1,0:T(8,128)(2,1)S(1)} %bitcast.949), channel_id=1, source_target_pairs={{0,1},{1,2},{2,3},{4,5},{5,6},{6,7},{8,9},{9,10},{10,11},{12,13},{... | collective-permute-start | bytes 6291464 | tf_op jit(solution)/shard_map/ppermute | solution.py:17
  29.0 3.4 %copy-start.2 = (bf16[8192,128]{1,0:T(8,128)(2,1)S(1)}, bf16[8192,128]{1,0:T(8,128)(2,1)}, u32[]{:S(2)}) copy-start(bf16[8192,128]{1,0:T(8,128)(2,1)} %get-tuple-element.94) | copy-start | bytes 6291460
  30.5 15.9 %slice-start = ((s8[8388608]{0:T(1024)(128)(4,1)}), s8[4194304]{0:T(1024)(128)(4,1)S(1)}, s32[]{:S(2)}) async-start(s8[8388608]{0:T(1024)(128)(4,1)} %bitcast.947), calls=%async_computation | async-start | bytes 8388608
  32.4 13.9 %slice-start.1 = ((s8[8388608]{0:T(1024)(128)(4,1)}), s8[4194304]{0:T(1024)(128)(4,1)S(1)}, s32[]{:S(2)}) async-start(s8[8388608]{0:T(1024)(128)(4,1)} %bitcast.947), calls=%async_computation.1 | async-start | bytes 8388608
  34.3 37.0 %collective-permute-start.2 = (bf16[2,2,1024,128]{3,2,1,0:T(8,128)(2,1)}, bf16[2,2,1024,128]{3,2,1,0:T(8,128)(2,1)S(1)}, u32[]{:S(2)}, u32[]{:S(2)}) collective-permute-start(bf16[2,2,1024,128]{3,2,1,0:T(8,128)(2,1)} %get-tuple-element.92), channel_id=1, source_target_pairs={{4,0},{8,4},{12,8},{16,12},{20,16},{24,20},{28,24},{32,28},{36,32}... | collective-permute-start | bytes 3145736 | tf_op jit(solution)/shard_map/ppermute | solution.py:30
  44.2 27.1 %collective-permute-start.1 = (bf16[2,2,1024,128]{3,2,1,0:T(8,128)(2,1)}, bf16[2,2,1024,128]{3,2,1,0:T(8,128)(2,1)}, u32[]{:S(2)}, u32[]{:S(2)}) collective-permute-start(bf16[2,2,1024,128]{3,2,1,0:T(8,128)(2,1)} %get-tuple-element.91), channel_id=1, source_target_pairs={{0,4},{4,8},{8,12},{12,16},{16,20},{20,24},{24,28},{28,32},{32,36}... | collective-permute-start | bytes 3145736 | tf_op jit(solution)/shard_map/ppermute | solution.py:28
  51.6 24.6 %copy-start.3 = (bf16[8192,128]{1,0:T(8,128)(2,1)S(1)}, bf16[8192,128]{1,0:T(8,128)(2,1)}, u32[]{:S(2)}) copy-start(bf16[8192,128]{1,0:T(8,128)(2,1)} %get-tuple-element.94) | copy-start | bytes 6291460
  76.1 4.6 %copy-start.5 = (bf16[16384,128]{1,0:T(8,128)(2,1)S(1)}, bf16[16384,128]{1,0:T(8,128)(2,1)}, u32[]{:S(2)}) copy-start(bf16[16384,128]{1,0:T(8,128)(2,1)} %copy-done.4) | copy-start | bytes 12582916
  97.3 43.2 %copy-start.7 = (pred[2,1,8,1024]{3,2,0,1:T(8,128)(4,1)S(1)}, pred[2,1,8,1024]{3,2,0,1:T(8,128)(4,1)}, u32[]{:S(2)}) copy-start(pred[2,1,8,1024]{3,2,0,1:T(8,128)(4,1)} %get-tuple-element.103) | copy-start | bytes 49156
  97.3 43.2 %copy-start.8 = (pred[2,1,8,1024]{3,2,0,1:T(8,128)(4,1)S(1)}, pred[2,1,8,1024]{3,2,0,1:T(8,128)(4,1)}, u32[]{:S(2)}) copy-start(pred[2,1,8,1024]{3,2,0,1:T(8,128)(4,1)} %get-tuple-element.104) | copy-start | bytes 49156
  97.3 63.5 %copy-start.12 = (f32[22]{0:T(128)S(1)}, f32[22]{0:T(128)}, u32[]{:S(2)}) copy-start(f32[22]{0:T(128)} %slice_multiply_fusion.1) | copy-start | bytes 268
  140.5 20.5 %copy-start.19 = (f32[20]{0:T(128)S(1)}, f32[20]{0:T(128)}, u32[]{:S(2)}) copy-start(f32[20]{0:T(128)} %slice.342) | copy-start | bytes 244
  140.5 20.9 %copy-start.18 = (f32[18]{0:T(128)S(1)}, f32[18]{0:T(128)}, u32[]{:S(2)}) copy-start(f32[18]{0:T(128)} %slice.350) | copy-start | bytes 220
  140.5 21.2 %copy-start.17 = (f32[16]{0:T(128)S(1)}, f32[16]{0:T(128)}, u32[]{:S(2)}) copy-start(f32[16]{0:T(128)} %slice.358) | copy-start | bytes 196
  140.5 21.5 %copy-start.16 = (f32[14]{0:T(128)S(1)}, f32[14]{0:T(128)}, u32[]{:S(2)}) copy-start(f32[14]{0:T(128)} %slice.366) | copy-start | bytes 172
  140.5 21.7 %copy-start.15 = (f32[12]{0:T(128)S(1)}, f32[12]{0:T(128)}, u32[]{:S(2)}) copy-start(f32[12]{0:T(128)} %slice.374) | copy-start | bytes 148
  141.2 21.3 %copy-start.14 = (f32[10]{0:T(128)S(1)}, f32[10]{0:T(128)}, u32[]{:S(2)}) copy-start(f32[10]{0:T(128)} %slice.382) | copy-start | bytes 124
  141.2 11.1 %collective-permute-start.4 = (bf16[2,3,8,1024]{3,2,1,0:T(8,128)(2,1)S(1)}, bf16[2,3,8,1024]{3,2,1,0:T(8,128)(2,1)S(1)}, u32[]{:S(2)}, u32[]{:S(2)}) collective-permute-start(bf16[2,3,8,1024]{3,2,1,0:T(8,128)(2,1)S(1)} %pad_maximum_fusion.3), channel_id=1, source_target_pairs={{4,0},{8,4},{12,8},{16,12},{20,16},{24,20},{28,24},{32,28},{36,32}... | collective-permute-start | bytes 294920 | tf_op jit(solution)/shard_map/ppermute | solution.py:30
  150.0 10.5 %collective-permute-start.3 = (bf16[2,3,8,1024]{3,2,1,0:T(8,128)(2,1)S(1)}, bf16[2,3,8,1024]{3,2,1,0:T(8,128)(2,1)S(1)}, u32[]{:S(2)}, u32[]{:S(2)}) collective-permute-start(bf16[2,3,8,1024]{3,2,1,0:T(8,128)(2,1)S(1)} %pad_maximum_fusion.3), channel_id=1, source_target_pairs={{0,4},{4,8},{8,12},{12,16},{16,20},{20,24},{24,28},{28,32},{32,36}... | collective-permute-start | bytes 294920 | tf_op jit(solution)/shard_map/ppermute | solution.py:28
  160.6 2.2 %copy-start.13 = (f32[8]{0:T(128)S(1)}, f32[8]{0:T(128)}, u32[]{:S(2)}) copy-start(f32[8]{0:T(128)} %slice.390) | copy-start | bytes 100
  160.8 41.1 %copy-start.10 = (f32[2,8,1024]{2,1,0:T(8,128)S(1)}, f32[2,8,1024]{2,1,0:T(8,128)}, u32[]{:S(2)}) copy-start(f32[2,8,1024]{2,1,0:T(8,128)} %param.14) | copy-start | bytes 196612
  160.8 41.1 %copy-start.20 = (f32[2,2,8,1024]{3,2,1,0:T(8,128)S(1)}, f32[2,2,8,1024]{3,2,1,0:T(8,128)}, u32[]{:S(2)}) copy-start(f32[2,2,8,1024]{3,2,1,0:T(8,128)} %custom-call) | copy-start | bytes 393220
  160.8 41.8 %copy-start.1 = (bf16[256,512]{1,0:T(8,128)(2,1)S(1)}, bf16[256,512]{1,0:T(8,128)(2,1)}, u32[]{:S(2)}) copy-start(bf16[256,512]{1,0:T(8,128)(2,1)} %param.15) | copy-start | bytes 786436
  201.9 0.7 copy-start.21
where the time goes:
time: 203 us
  other arithmetic  87.3 us (43%)
  blocking collectives  38.8 us (19%)
  waiting for transfers between devices  28 us (14%)
  starting transfers between devices  24.2 us (12%)
  matrix products  13.5 us (7%)
  local copies, waits for them, and re-layouts  9.92 us (5%)
    reduce_sum x3, other arithmetic, flow_field(): jnp.sum(own * window.astype(jnp.float32), axis=-1) / own.shape[-1]  64.9 us
    all_gather x1, blocking collectives, entering(): lax.all_gather(value.astype(jnp.bfloat16 if value.dtype == jnp.float32 el...  38.8 us
    ppermute x2, waiting for transfers between devices, with_halo(): lax.ppermute(head, axis, [((i + 1) % count, i) for i in range(ends)])  19.8 us
    ppermute x2, starting transfers between devices, with_halo(): lax.ppermute(head, axis, [((i + 1) % count, i) for i in range(ends)])  18.7 us
    dot_general x1, matrix products, encode(): pre = jnp.dot(hidden, w_feature, preferred_element_type=jnp.float32)  13.5 us
    concatenate x2, other arithmetic, with_halo(): jnp.concatenate([lax.ppermute(tail, axis, [(i, (i + 1) % count) for i in...  9.31 us
    ppermute x2, waiting for transfers between devices, with_halo(): lax.ppermute(tail, axis, [(i, (i + 1) % count) for i in range(ends)])  8.25 us
    convert_element_type x1, other arithmetic, encode(): result = (pre * scale * feat_gain).astype(jnp.bfloat16)  5.28 us
  transfers between devices with their start and end apart: 5, of which 2 were waited for; matrix products, arithmetic and copies ran while one was open for 5% of the time, Pallas kernels for 0%

commit v1 on v0

v1 whole, which is shorter than its diff:
```python
import jax
import jax.numpy as jnp
from jax import lax
from jax.experimental import pallas as pl
from jax.experimental.pallas import tpu as pltpu
from jax.sharding import PartitionSpec as P

MESH = pl.DeviceIdType.MESH
ITERS = 8
COLS = 1024
PAD = 16
WIDE = COLS + 2 * PAD
HALF = COLS // 2
REACH = 8
ROWS = 8
ALL = ROWS + 2 * REACH
EPS = 1e-05


def remote(src, dst, send, recv, device):
    return pltpu.make_async_remote_copy(
        src_ref=src, dst_ref=dst, send_sem=send, recv_sem=recv, device_id=device, device_id_type=MESH
    )


def body(
    pix_hbm, pred_hbm, offs, mask, w1, w2, gain, out,
    pix, fp, fa, fb, rel, msend, mrecv, flow, fsend, frecv, psend, precv,
    pix_sem, pred_sem, sec_s, sec_r, halo_s, halo_r, rel_s, rel_r, m_s, m_r, f_s, f_r, p_s, p_r,
):
    t = lax.axis_index("tile")
    s = lax.axis_index("sec")
    tiles = lax.axis_size("tile")
    last = tiles - 1
    y = lax.rem(t, 4)
    low = y == 0
    high = y == 3
    has_d = t < last
    has_u = t > 0
    td = jnp.minimum(t + 1, last)
    tu = jnp.maximum(t - 1, 0)
    out_ok = (high & has_d) | (low & has_u)
    rel_dev = jnp.where(high, t - 3, jnp.minimum(t + 3, last))
    in_ok = (high & (rel_dev > 0)) | (low & (rel_dev < last))
    rel_dst = jnp.where(high, jnp.maximum(t - 4, 0), jnp.minimum(t + 4, last))
    fwd = jnp.where(high, jnp.minimum(t + 4, last), jnp.maximum(t - 4, 0))
    next_sec = jnp.minimum(s + 1, 3)

    for q in (1, 0):
        for r in range(ROWS):
            pltpu.make_async_copy(pix_hbm.at[q, r], pix.at[q, r], pix_sem.at[q, r]).start()
    pred_copy = pltpu.make_async_copy(
        pred_hbm, fp.at[pl.ds(2, ROWS), pl.ds(PAD, COLS)], pred_sem
    )

    @pl.when(s == 0)
    def _():
        pred_copy.start()

    zero_side = jnp.zeros((ROWS + 4, PAD, 128), jnp.bfloat16)
    for f in (fp, fa):
        f[:, pl.ds(0, PAD), :] = zero_side
        f[:, pl.ds(PAD + COLS, PAD), :] = zero_side
    zero_rows = jnp.zeros((2, COLS, 128), jnp.bfloat16)

    @pl.when(jnp.logical_not(has_u))
    def _():
        for f in (fp, fa):
            f[pl.ds(0, 2), pl.ds(PAD, COLS), :] = zero_rows
        mrecv[0] = jnp.zeros((16, COLS), jnp.bfloat16)
        for q in range(2):
            frecv[q, 0] = jnp.zeros((16, COLS), jnp.bfloat16)

    @pl.when(jnp.logical_not(has_d))
    def _():
        for f in (fp, fa):
            f[pl.ds(ROWS + 2, 2), pl.ds(PAD, COLS), :] = zero_rows
        mrecv[1] = jnp.zeros((16, COLS), jnp.bfloat16)
        for q in range(2):
            frecv[q, 1] = jnp.zeros((16, COLS), jnp.bfloat16)

    msend[...] = jnp.concatenate([mask[0], mask[1]], axis=0).astype(jnp.float32).astype(jnp.bfloat16)

    barrier = pltpu.get_barrier_semaphore()
    count = jnp.int32(0)
    for ok, device in (
        (has_d, (td, s)),
        (has_u, (tu, s)),
        (out_ok | in_ok, (rel_dev, s)),
        (in_ok, (rel_dst, s)),
        (out_ok, (fwd, s)),
    ):
        count = count + ok.astype(jnp.int32)

        @pl.when(ok)
        def _(device=device):
            pl.semaphore_signal(barrier, inc=1, device_id=device, device_id_type=MESH)

    for k in range(1, 4):
        pl.semaphore_signal(
            barrier, inc=1, device_id=(t, lax.rem(s + k, 4)), device_id_type=MESH
        )
    pl.semaphore_wait(barrier, count + 3)

    def mask_copy(d):
        return remote(msend, mrecv.at[d], m_s.at[d], m_r.at[d], ((td, tu)[d], s))

    def flow_copy(q, d):
        return remote(fsend.at[q], frecv.at[q, d], f_s.at[q, d], f_r.at[q, d], ((td, tu)[d], s))

    def sec_copy(r):
        span = (r + 2, pl.ds(PAD, COLS))
        return remote(fb.at[span], fp.at[span], sec_s.at[r], sec_r.at[r], (t, next_sec))

    feats = (fp, fa)

    def halo_src(u, d, h):
        return feats[u].at[pl.ds(ROWS if d == 0 else 2, 2), pl.ds(PAD + h * HALF, HALF)]

    def halo_dst(u, d, h):
        return feats[u].at[pl.ds(0 if d == 0 else ROWS + 2, 2), pl.ds(PAD + h * HALF, HALF)]

    def direct(u, d, h):
        return remote(
            halo_src(u, d, h), halo_dst(u, d, h), halo_s.at[u, d, h], halo_r.at[u, d, h],
            ((td, tu)[d], s),
        )

    def to_relay(u, d):
        return remote(
            halo_src(u, d, 1), rel.at[u], halo_s.at[u, d, 1], rel_r.at[u], (rel_dev, s)
        )

    def from_relay(u, d):
        return remote(
            rel.at[u], halo_dst(u, d, 1), rel_s.at[u], halo_r.at[u, d, 1], (rel_dst, s)
        )

    ends = (high, low)
    has = (has_d, has_u)

    def start_halo(u):
        for d in range(2):
            edge = ends[d] & has[d]

            @pl.when(edge)
            def _(d=d):
                to_relay(u, d).start()

        for d in range(2):
            edge = ends[d] & has[d]

            @pl.when(has[d])
            def _(d=d):
                direct(u, d, 0).start()

            @pl.when(has[d] & jnp.logical_not(edge))
            def _(d=d):
                direct(u, d, 1).start()

    def relay(u):
        for d in range(2):

            @pl.when(ends[1 - d] & in_ok)
            def _(d=d):
                to_relay(u, d).wait_recv()
                from_relay(u, d).start()

    def wait_halo(u):
        for d in range(2):

            @pl.when(has[1 - d])
            def _(d=d):
                direct(u, d, 0).wait_recv()
                direct(u, d, 1).wait_recv()

    def drain_halo(u):
        for d in range(2):

            @pl.when(has[d])
            def _(d=d):
                direct(u, d, 0).wait_send()
                direct(u, d, 1).wait_send()

            @pl.when(ends[1 - d] & in_ok)
            def _(d=d):
                from_relay(u, d).wait_send()

    for d in range(2):

        @pl.when(has[d])
        def _(d=d):
            mask_copy(d).start()

    @pl.when(s == 0)
    def _():
        pred_copy.wait()
        start_halo(0)

    def encode_row(q, f, r):
        pltpu.make_async_copy(pix_hbm.at[q, r], pix.at[q, r], pix_sem.at[q, r]).wait()

        def block(b, carry):
            x = pix[q, r, pl.ds(pl.multiple_of(b * 256, 256), 256), :]
            hidden = jnp.maximum(
                jnp.dot(x, w1[...], preferred_element_type=jnp.float32), 0.0
            ).astype(jnp.bfloat16)
            pre = jnp.dot(hidden, w2[...], preferred_element_type=jnp.float32)
            scale = lax.rsqrt(jnp.mean(pre * pre, axis=-1, keepdims=True) + EPS)
            f[r + 2, pl.ds(pl.multiple_of(PAD + b * 256, 16), 256), :] = (
                pre * scale * gain[...]
            ).astype(jnp.bfloat16)
            return carry

        lax.fori_loop(0, COLS // 256, block, 0)

    def outer_row(i):
        return jnp.where(i < 2, i, i + 4)

    def encode_last(i, carry):
        r = jnp.where(i < 4, outer_row(i), i - 2)
        encode_row(1, fb, r)

        @pl.when(s < 3)
        def _():
            sec_copy(r).start()

        return carry

    lax.fori_loop(0, ROWS, encode_last, 0)

    @pl.when(s == 0)
    def _():
        relay(0)

    def encode_outer(i, carry):
        encode_row(0, fa, outer_row(i))
        return carry

    def encode_inner(i, carry):
        encode_row(0, fa, i + 2)
        return carry

    lax.fori_loop(0, 4, encode_outer, 0)
    start_halo(1)
    lax.fori_loop(0, 4, encode_inner, 0)

    @pl.when(s > 0)
    def _():
        for r in (0, 1, 6, 7):
            sec_copy(r).wait_recv()
        start_halo(0)

    relay(1)

    sub = lax.broadcasted_iota(jnp.int32, (8, 128), 0)
    lane = lax.broadcasted_iota(jnp.int32, (8, 128), 1)
    turn = lane + (PAD - 2)
    which = (turn + ((sub - turn) & 7)) // 8

    def diagonals(g):
        picked = g[8:16]
        for k in range(2, 19):
            picked = jnp.where(which == k, g[8 * k : 8 * k + 8], picked)
        return picked

    def score_block(q, own, ref, pair, c):
        c0 = pl.multiple_of(c * 128, 128)
        r0 = pair * 2
        rhs = own[pl.ds(r0 + 2, 2), pl.ds(pl.multiple_of(c0 + PAD, 16), 128), :].reshape(256, 128)
        bands = ([], [])
        for k in range(6):
            lhs = ref[r0 + k, pl.ds(c0, 160), :]
            g = lax.dot_general(
                lhs, rhs, (((1,), (1,)), ((), ())), preferred_element_type=jnp.float32
            )
            for j in range(2):
                if 0 <= k - j <= 4:
                    bands[j].append(diagonals(g[:, 128 * j : 128 * j + 128]))
        for j in range(2):
            r = r0 + j
            oy = jnp.broadcast_to(offs[q, 0, pl.ds(r, 1), pl.ds(c0, 128)], (8, 128))
            ox = jnp.broadcast_to(offs[q, 1, pl.ds(r, 1), pl.ds(c0, 128)], (8, 128))
            spin = turn + ox + 1
            band = bands[j]
            for bit in (1, 2, 4):
                take = (spin & bit) != 0
                band = [jnp.where(take, pltpu.roll(v, 8 - bit, 0), v) for v in band]
            weights = []
            for i in range(3):
                near = jnp.where(oy < 0, band[i], jnp.where(oy == 0, band[i + 1], band[i + 2]))
                weights.append(near * near * (2.0**-14))
            every = weights[0] + weights[1] + weights[2]
            tilt = weights[2] - weights[0]
            every1 = pltpu.roll(every, 7, 0)
            every2 = pltpu.roll(every, 6, 0)
            total = 1.0 + (every + every1 + every2)
            sum_y = tilt + pltpu.roll(tilt, 7, 0) + pltpu.roll(tilt, 6, 0)
            sum_x = every2 - every
            flow_y = oy.astype(jnp.float32) + sum_y / total
            flow_x = ox.astype(jnp.float32) + sum_x / total
            flow[q, 0, pl.ds(REACH + r, 1), pl.ds(c0, 128)] = flow_y[0:1]
            flow[q, 1, pl.ds(REACH + r, 1), pl.ds(c0, 128)] = flow_x[0:1]

    def score_pairs(q, own, ref, pairs):
        for pair in pairs:

            def one(c, carry, pair=pair):
                score_block(q, own, ref, pair, c)
                return carry

            lax.fori_loop(0, COLS // 128, one, 0)

    def send_flow(q):
        fsend[q] = jnp.concatenate(
            [flow[q, 0, pl.ds(REACH, ROWS), :], flow[q, 1, pl.ds(REACH, ROWS), :]], axis=0
        ).astype(jnp.bfloat16)
        for d in range(2):

            @pl.when(has[d])
            def _(d=d):
                flow_copy(q, d).start()

    score_pairs(1, fb, fa, (1, 2))

    @pl.when(s > 0)
    def _():
        relay(0)
        for r in (2, 3, 4, 5):
            sec_copy(r).wait_recv()

    score_pairs(0, fa, fp, (1, 2))
    wait_halo(1)
    score_pairs(1, fb, fa, (0, 3))
    send_flow(1)
    wait_halo(0)
    score_pairs(0, fa, fp, (0, 3))
    send_flow(0)

    for d in range(2):

        @pl.when(has[1 - d])
        def _(d=d):
            mask_copy(d).wait_recv()

    row = lax.broadcasted_iota(jnp.int32, (ALL, COLS), 0) + t * ROWS - REACH
    col = lax.broadcasted_iota(jnp.int32, (ALL, COLS), 1)
    inside = jnp.where((row >= 0) & (row < tiles * ROWS), 0.2, 0.0)
    left_ok = jnp.where(col > 0, 1.0, 0.0)
    right_ok = jnp.where(col < COLS - 1, 1.0, 0.0)
    for q in (1, 0):
        for d in range(2):

            @pl.when(has[1 - d])
            def _(q=q, d=d):
                flow_copy(q, d).wait_recv()

        trust = jnp.concatenate(
            [
                mrecv[0, pl.ds(8 * q, 8), :].astype(jnp.float32),
                mask[q].astype(jnp.float32),
                mrecv[1, pl.ds(8 * q, 8), :].astype(jnp.float32),
            ],
            axis=0,
        ) * 0.5
        keep = inside * (1.0 - trust)
        for comp in range(2):
            target = jnp.concatenate(
                [
                    frecv[q, 0, pl.ds(8 * comp, 8), :].astype(jnp.float32),
                    flow[q, comp, pl.ds(REACH, ROWS), :],
                    frecv[q, 1, pl.ds(8 * comp, 8), :].astype(jnp.float32),
                ],
                axis=0,
            )
            drive = inside * trust * target

            def relax(i, field):
                sides = pltpu.roll(field, 1, 1) * left_ok + pltpu.roll(field, COLS - 1, 1) * right_ok
                around = pltpu.roll(field, 1, 0) + pltpu.roll(field, ALL - 1, 0) + sides
                return inside * around + keep * field + drive

            field = lax.fori_loop(1, ITERS, relax, drive)
            flow[q, comp] = field

    mine = pl.ds(REACH, ROWS)
    psend[...] = jnp.concatenate(
        [flow[0, 0, mine, :] + flow[1, 0, mine, :], flow[0, 1, mine, :] + flow[1, 1, mine, :]], axis=0
    ).astype(jnp.bfloat16)

    def prefix_copy(k):
        return remote(
            psend, precv.at[jnp.minimum(s, 2)], p_s.at[k - 1], p_r.at[jnp.minimum(s, 2)],
            (t, jnp.minimum(s + k, 3)),
        )

    for k in (1, 2, 3):

        @pl.when(s + k <= 3)
        def _(k=k):
            prefix_copy(k).start()

    for comp in range(2):
        out[0, comp] = flow[0, comp, mine, :]
        out[1, comp] = flow[0, comp, mine, :] + flow[1, comp, mine, :]

    for source in range(3):

        @pl.when(s > source)
        def _(source=source):
            remote(
                psend, precv.at[source], p_s.at[0], p_r.at[source], (t, next_sec)
            ).wait_recv()
            for comp in range(2):
                add = precv[source, pl.ds(8 * comp, 8), :].astype(jnp.float32)
                for q in range(2):
                    out[q, comp] = out[q, comp] + add

    for d in range(2):

        @pl.when(has[d])
        def _(d=d):
            mask_copy(d).wait_send()
            for q in range(2):
                flow_copy(q, d).wait_send()

    for u in range(2):
        drain_halo(u)

    @pl.when(s < 3)
    def _():
        for r in range(ROWS):
            sec_copy(r).wait_send()

    for k in (1, 2, 3):

        @pl.when(s + k <= 3)
        def _(k=k):
            prefix_copy(k).wait_send()


def shards(pixels, pred_features, offsets, valid_mask, base_shift, w_hidden, w_feature, feat_gain):
    vm = pl.BlockSpec(memory_space=pltpu.VMEM)
    hbm = pl.BlockSpec(memory_space=pl.ANY)
    dma = pltpu.SemaphoreType.DMA
    bf = jnp.bfloat16
    summed = pl.pallas_call(
        body,
        out_shape=jax.ShapeDtypeStruct((2, 2, ROWS, COLS), jnp.float32),
        in_specs=[hbm, hbm, vm, vm, vm, vm, vm],
        out_specs=vm,
        scratch_shapes=[
            pltpu.VMEM((2, ROWS, COLS, 256), bf),
            pltpu.VMEM((ROWS + 4, WIDE, 128), bf),
            pltpu.VMEM((ROWS + 4, WIDE, 128), bf),
            pltpu.VMEM((ROWS + 4, WIDE, 128), bf),
            pltpu.VMEM((2, 2, HALF, 128), bf),
            pltpu.VMEM((16, COLS), bf),
            pltpu.VMEM((2, 16, COLS), bf),
            pltpu.VMEM((2, 2, ALL, COLS), jnp.float32),
            pltpu.VMEM((2, 16, COLS), bf),
            pltpu.VMEM((2, 2, 16, COLS), bf),
            pltpu.VMEM((16, COLS), bf),
            pltpu.VMEM((3, 16, COLS), bf),
            dma((2, ROWS)),
            dma,
            dma((ROWS,)),
            dma((ROWS,)),
            dma((2, 2, 2)),
            dma((2, 2, 2)),
            dma((2,)),
            dma((2,)),
            dma((2,)),
            dma((2,)),
            dma((2, 2)),
            dma((2, 2)),
            dma((3,)),
            dma((3,)),
        ],
        compiler_params=pltpu.CompilerParams(
            collective_id=0, has_side_effects=True, vmem_limit_bytes=48 << 20
        ),
        name="align",
    )(
        pixels, pred_features, offsets, valid_mask, w_hidden, w_feature, feat_gain.reshape(1, 128)
    )
    return summed + base_shift[None]


def solution(mesh):
    in_specs = (
        P("sec", "tile", None, None),
        P("tile", None, None),
        P("sec", None, "tile", None),
        P("sec", "tile", None),
        P(None, "tile", None),
        P(),
        P(),
        P(),
    )
    out_specs = P("sec", None, "tile", None)
    return jax.shard_map(shards, mesh=mesh, in_specs=in_specs, out_specs=out_specs, check_vma=False)
```

time: 203 us -> 84.6 us (0.42)
  other arithmetic: 87.3 us -> 0.67 us
  Pallas kernels: 0 us -> 77.8 us
  blocking collectives: 38.8 us -> 0 us
  waiting for transfers between devices: 28 us -> 0 us
  starting transfers between devices: 24.2 us -> 0 us
  matrix products: 13.5 us -> 0 us
  local copies, waits for them, and re-layouts: 9.92 us -> 5.84 us
    pallas_call x0 -> x1, Pallas kernels: none -> 77.8 us  [shards(): pl.pallas_call(body, out_shape=jax.ShapeDtypeStruct((2, 2, ROWS, COLS), j...]
    reduce_sum x4 -> x0, other arithmetic: 65.1 us -> none  [the longest x3 64.9 us: flow_field(): jnp.sum(own * window.astype(jnp.float32), axis=-1) / own.shape[-1]]
    all_gather x1 -> x0, blocking collectives: 38.8 us -> none  [entering(): lax.all_gather(value.astype(jnp.bfloat16 if value.dtype == jnp.float32 el...]
    ppermute x5 -> x0, waiting for transfers between devices: 28 us -> none  [the longest x2 19.8 us: with_halo(): lax.ppermute(head, axis, [((i + 1) % count, i) for i in range(ends)])]
    ppermute x5 -> x0, starting transfers between devices: 24.2 us -> none  [the longest x2 18.7 us: with_halo(): lax.ppermute(head, axis, [((i + 1) % count, i) for i in range(ends)])]
    dot_general x1 -> x0, matrix products: 13.5 us -> none  [encode(): pre = jnp.dot(hidden, w_feature, preferred_element_type=jnp.float32)]
    concatenate x5 -> x0, other arithmetic: 11.2 us -> none  [the longest x2 9.31 us: with_halo(): jnp.concatenate([lax.ppermute(tail, axis, [(i, (i + 1) % count) for i in...]
    slice x16 -> x0, local copies, waits for them, and re-layouts: 6.15 us -> none  [the longest x7 4.3 us: shards(): inside[start:start + length][None, None, :, None]]
  transfers between devices with their start and end apart: 5 -> 0, of which waited for: 2 -> 0; matrix products, arithmetic and copies ran while one was open for 5% -> 0% of each run, Pallas kernels for 0% -> 0%
where the time goes in v1:
time: 84.6 us; the launch traced here: 84.3 us
  Pallas kernels  77.8 us (92%)
  local copies, waits for them, and re-layouts  5.84 us (7%)
    pallas_call x1, Pallas kernels, shards(): pl.pallas_call(body, out_shape=jax.ShapeDtypeStruct((2, 2, ROWS, COLS), j...  77.8 us
    unnamed x14, local copies, waits for them, and re-layouts  5.84 us

profile of v1, /device:TPU:39, one launch (start us, length us, event | category | flops | bytes accessed | tf_op | source)
XLA Modules:
  0.0 84.3 jit_solution(14030790914536189783)
XLA Ops:
  0.0 0.0 copy-start
  0.0 1.6 %copy-done = bf16[8,1024,128]{2,1,0:T(8,128)(2,1)S(1)} copy-done((bf16[8,1024,128]{2,1,0:T(8,128)(2,1)S(1)}, bf16[8,1024,128]{2,1,0:T(8,128)(2,1)}, u32[]{:S(2)}) %copy-start) | copy-done | bytes 2097176
  1.6 0.0 copy-start.1
  1.6 0.9 %copy-done.1 = bf16[256,512]{1,0:T(8,128)(2,1)S(1)} copy-done((bf16[256,512]{1,0:T(8,128)(2,1)S(1)}, bf16[256,512]{1,0:T(8,128)(2,1)}, u32[]{:S(2)}) %copy-start.1) | copy-done | bytes 262168
  2.5 0.0 copy-start.2
  2.5 0.9 %copy-done.2 = s32[2,2,8,1024]{3,2,1,0:T(8,128)S(1)} copy-done((s32[2,2,8,1024]{3,2,1,0:T(8,128)S(1)}, s32[2,2,8,1024]{3,2,1,0:T(8,128)}, u32[]{:S(2)}) %copy-start.2) | copy-done | bytes 131096
  3.4 0.0 copy-start.3
  3.4 0.9 %copy-done.3 = bf16[512,128]{1,0:T(8,128)(2,1)S(1)} copy-done((bf16[512,128]{1,0:T(8,128)(2,1)S(1)}, bf16[512,128]{1,0:T(8,128)(2,1)}, u32[]{:S(2)}) %copy-start.3) | copy-done | bytes 131096
  4.4 0.0 copy-start.4
  4.4 0.8 copy-done.4
  5.2 0.0 copy-start.5
  5.2 0.7 copy-done.5
  5.8 0.0 copy-start.6
  5.8 77.8 %align.1 = f32[2,2,8,1024]{3,2,1,0:T(8,128)S(1)} custom-call(bf16[2,8,1024,256]{3,2,1,0:T(8,128)(2,1)} %pix_hbm.1, bf16[8,1024,128]{2,1,0:T(8,128)(2,1)S(1)} %copy-done, s32[2,2,8,1024]{3,2,1,0:T(8,128)S(1)} %copy-done.2, s32[2,8,1024]{2,1,0:T(8,128)S(1)} %copy-done.4, bf16[256,512]{1,0:T(8,128)(2,1)S(1)} %copy-done.1, bf16[512,128]{1,0:T(8,128)(2,1)S(1)} %copy-done.3, ...), custom_call_target="tpu_custom_call" | custom-call | tf_op jit(solution)/shard_map/align/pallas_call | solution.py:447
  83.7 0.0 copy-done.6
  83.7 0.7 broadcast_add_fusion
Async XLA Ops:
  0.0 1.6 %copy-start = (bf16[8,1024,128]{2,1,0:T(8,128)(2,1)S(1)}, bf16[8,1024,128]{2,1,0:T(8,128)(2,1)}, u32[]{:S(2)}) copy-start(bf16[8,1024,128]{2,1,0:T(8,128)(2,1)} %pred_hbm.1) | copy-start | bytes 6291460
  1.6 0.9 %copy-start.1 = (bf16[256,512]{1,0:T(8,128)(2,1)S(1)}, bf16[256,512]{1,0:T(8,128)(2,1)}, u32[]{:S(2)}) copy-start(bf16[256,512]{1,0:T(8,128)(2,1)} %w1.1) | copy-start | bytes 786436
  2.5 0.9 %copy-start.2 = (s32[2,2,8,1024]{3,2,1,0:T(8,128)S(1)}, s32[2,2,8,1024]{3,2,1,0:T(8,128)}, u32[]{:S(2)}) copy-start(s32[2,2,8,1024]{3,2,1,0:T(8,128)} %offs.1) | copy-start | bytes 393220
  3.4 0.9 %copy-start.3 = (bf16[512,128]{1,0:T(8,128)(2,1)S(1)}, bf16[512,128]{1,0:T(8,128)(2,1)}, u32[]{:S(2)}) copy-start(bf16[512,128]{1,0:T(8,128)(2,1)} %w2.1) | copy-start | bytes 393220
  4.4 0.8 copy-start.4
  5.2 0.7 copy-start.5
  5.8 77.8 %copy-start.6 = (f32[2,8,1024]{2,1,0:T(8,128)S(1)}, f32[2,8,1024]{2,1,0:T(8,128)}, u32[]{:S(2)}) copy-start(f32[2,8,1024]{2,1,0:T(8,128)} %param.12) | copy-start | bytes 196612

commit v2 on v1

--- a/solution.py
+++ b/solution.py
@@ -11,6 +11,11 @@
 PAD = 16
 WIDE = COLS + 2 * PAD
 HALF = COLS // 2
+SPANS = {
+    "full": ((PAD, HALF), (PAD + HALF, HALF)),
+    "left": ((PAD, 272), (PAD + 272, 256)),
+    "right": ((HALF, 272), (HALF + 272, 256)),
+}
 REACH = 8
 ROWS = 8
 ALL = ROWS + 2 * REACH
@@ -24,9 +29,9 @@
 
 
 def body(
-    pix_hbm, pred_hbm, offs, mask, w1, w2, gain, out,
-    pix, fp, fa, fb, rel, msend, mrecv, flow, fsend, frecv, psend, precv,
-    pix_sem, pred_sem, sec_s, sec_r, halo_s, halo_r, rel_s, rel_r, m_s, m_r, f_s, f_r, p_s, p_r,
+    pix_hbm, pred_hbm, offs_hbm, mask_hbm, w1_hbm, w2_hbm, gain_hbm, out,
+    offs, mask, w1, w2, gain, pix, fp, fa, fb, ga, goffs, gflow, bsend, brecv, rel, msend, mrecv, flow, fsend, frecv, psend, precv,
+    in_sem, pix_sem, pred_sem, sec_s, sec_r, halo_s, halo_r, rel_s, rel_r, m_s, m_r, f_s, f_r, p_s, p_r, g_s, g_r, x_s, x_r, b_s, b_r,
 ):
     t = lax.axis_index("tile")
     s = lax.axis_index("sec")
@@ -46,39 +51,55 @@
     fwd = jnp.where(high, jnp.minimum(t + 4, last), jnp.maximum(t - 4, 0))
     next_sec = jnp.minimum(s + 1, 3)
 
-    for q in (1, 0):
-        for r in range(ROWS):
+    small = [
+        pltpu.make_async_copy(src, dst, in_sem.at[i])
+        for i, (src, dst) in enumerate(
+            (
+                (mask_hbm, mask), (w1_hbm, w1), (w2_hbm, w2), (gain_hbm, gain), (offs_hbm, offs),
+            )
+        )
+    ]
+    for copy in small[:4]:
+        copy.start()
+    outer, inner = (0, 1, 6, 7), (2, 3, 4, 5)
+    for q, rows in ((0, outer), (1, outer), (1, inner), (0, inner)):
+        for r in rows:
             pltpu.make_async_copy(pix_hbm.at[q, r], pix.at[q, r], pix_sem.at[q, r]).start()
     pred_copy = pltpu.make_async_copy(
         pred_hbm, fp.at[pl.ds(2, ROWS), pl.ds(PAD, COLS)], pred_sem
     )
 
+    small[4].start()
+
     @pl.when(s == 0)
     def _():
         pred_copy.start()
 
     zero_side = jnp.zeros((ROWS + 4, PAD, 128), jnp.bfloat16)
-    for f in (fp, fa):
+    for f in (fp, fa, fb):
         f[:, pl.ds(0, PAD), :] = zero_side
         f[:, pl.ds(PAD + COLS, PAD), :] = zero_side
     zero_rows = jnp.zeros((2, COLS, 128), jnp.bfloat16)
 
     @pl.when(jnp.logical_not(has_u))
     def _():
-        for f in (fp, fa):
+        for f in (fp, fa, fb):
             f[pl.ds(0, 2), pl.ds(PAD, COLS), :] = zero_rows
         mrecv[0] = jnp.zeros((16, COLS), jnp.bfloat16)
+        brecv[0] = jnp.zeros((8, COLS), jnp.bfloat16)
         for q in range(2):
             frecv[q, 0] = jnp.zeros((16, COLS), jnp.bfloat16)
 
     @pl.when(jnp.logical_not(has_d))
     def _():
-        for f in (fp, fa):
+        for f in (fp, fa, fb):
             f[pl.ds(ROWS + 2, 2), pl.ds(PAD, COLS), :] = zero_rows
         mrecv[1] = jnp.zeros((16, COLS), jnp.bfloat16)
+        brecv[1] = jnp.zeros((8, COLS), jnp.bfloat16)
         for q in range(2):
             frecv[q, 1] = jnp.zeros((16, COLS), jnp.bfloat16)
 
+    small[0].wait()
     msend[...] = jnp.concatenate([mask[0], mask[1]], axis=0).astype(jnp.float32).astype(jnp.bfloat16)
 
     barrier = pltpu.get_barrier_semaphore()
@@ -105,86 +126,122 @@
     def mask_copy(d):
         return remote(msend, mrecv.at[d], m_s.at[d], m_r.at[d], ((td, tu)[d], s))
 
+    def band_copy(d):
+        return remote(bsend.at[d], brecv.at[d], b_s.at[d], b_r.at[d], ((td, tu)[d], s))
+
     def flow_copy(q, d):
         return remote(fsend.at[q], frecv.at[q, d], f_s.at[q, d], f_r.at[q, d], ((td, tu)[d], s))
 
-    def sec_copy(r):
-        span = (r + 2, pl.ds(PAD, COLS))
-        return remote(fb.at[span], fp.at[span], sec_s.at[r], sec_r.at[r], (t, next_sec))
-
-    feats = (fp, fa)
-
-    def halo_src(u, d, h):
-        return feats[u].at[pl.ds(ROWS if d == 0 else 2, 2), pl.ds(PAD + h * HALF, HALF)]
-
-    def halo_dst(u, d, h):
-        return feats[u].at[pl.ds(0 if d == 0 else ROWS + 2, 2), pl.ds(PAD + h * HALF, HALF)]
-
-    def direct(u, d, h):
+    def sec_copy(r, h):
+        span = (r + 2, pl.ds(PAD, HALF + PAD) if h == 0 else pl.ds(HALF + 2 * PAD, HALF - PAD))
+        return remote(fb.at[span], fp.at[span], sec_s.at[r, h], sec_r.at[r, h], (t, next_sec))
+
+    def give_rows(r):
         return remote(
-            halo_src(u, d, h), halo_dst(u, d, h), halo_s.at[u, d, h], halo_r.at[u, d, h],
+            fa.at[r + 2, pl.ds(PAD + HALF, HALF)], ga.at[r], g_s.at[r], g_r.at[r], (t, 1)
+        )
+
+    def give_offs():
+        return remote(
+            offs.at[0, :, :, pl.ds(HALF, HALF)], goffs, x_s.at[0], x_r.at[0], (t, 1)
+        )
+
+    def give_flow():
+        return remote(
+            gflow, flow.at[0, :, pl.ds(REACH, ROWS), pl.ds(HALF, HALF)], x_s.at[1], x_r.at[1], (t, 2)
+        )
+
+    feats = (fp, fa, fb)
+
+    deep = (1, 2, 2)
+
+    def halo_src(u, d, span):
+        return feats[u].at[pl.ds(ROWS + 2 - deep[u] if d == 0 else 2, deep[u]), pl.ds(*span)]
+
+    def halo_dst(u, d, span):
+        return feats[u].at[pl.ds(2 - deep[u] if d == 0 else ROWS + 2, deep[u]), pl.ds(*span)]
+
+    def direct(u, d, h, kind):
+        span = SPANS[kind][h]
+        return remote(
+            halo_src(u, d, span), halo_dst(u, d, span), halo_s.at[u, d, h], halo_r.at[u, d, h],
             ((td, tu)[d], s),
         )
 
-    def to_relay(u, d):
+    def to_relay(u, d, kind):
+        span = SPANS[kind][1]
         return remote(
-            halo_src(u, d, 1), rel.at[u], halo_s.at[u, d, 1], rel_r.at[u], (rel_dev, s)
-        )
-
-    def from_relay(u, d):
+            halo_src(u, d, span), rel.at[u, pl.ds(0, deep[u]), pl.ds(0, span[1])], halo_s.at[u, d, 1], rel_r.at[u],
+            (rel_dev, s),
+        )
+
+    def from_relay(u, d, kind):
+        span = SPANS[kind][1]
         return remote(
-            rel.at[u], halo_dst(u, d, 1), rel_s.at[u], halo_r.at[u, d, 1], (rel_dst, s)
+            rel.at[u, pl.ds(0, deep[u]), pl.ds(0, span[1])], halo_dst(u, d, span), rel_s.at[u], halo_r.at[u, d, 1],
+            (rel_dst, s),
         )
 
     ends = (high, low)
     has = (has_d, has_u)
 
-    def start_halo(u):
+    def start_halo(u, kind="full"):
         for d in range(2):
             edge = ends[d] & has[d]
 
             @pl.when(edge)
             def _(d=d):
-                to_relay(u, d).start()
+                to_relay(u, d, kind).start()
 
         for d in range(2):
             edge = ends[d] & has[d]
 
             @pl.when(has[d])
             def _(d=d):
-                direct(u, d, 0).start()
+                direct(u, d, 0, kind).start()
 
             @pl.when(has[d] & jnp.logical_not(edge))
             def _(d=d):
-                direct(u, d, 1).start()
-
-    def relay(u):
+                direct(u, d, 1, kind).start()
+
+    def relay(u, kind="full"):
         for d in range(2):
 
             @pl.when(ends[1 - d] & in_ok)
             def _(d=d):
-                to_relay(u, d).wait_recv()
-                from_relay(u, d).start()
-
-    def wait_halo(u):
+                to_relay(u, d, kind).wait_recv()
+                from_relay(u, d, kind).start()
+
+    def wait_halo(u, kind="full"):
         for d in range(2):
 
             @pl.when(has[1 - d])
             def _(d=d):
-                direct(u, d, 0).wait_recv()
-                direct(u, d, 1).wait_recv()
-
-    def drain_halo(u):
+                direct(u, d, 0, kind).wait_recv()
+                direct(u, d, 1, kind).wait_recv()
+
+    def drain_halo(u, kind="full"):
         for d in range(2):
 
             @pl.when(has[d])
             def _(d=d):
-                direct(u, d, 0).wait_send()
-                direct(u, d, 1).wait_send()
+                direct(u, d, 0, kind).wait_send()
+                direct(u, d, 1, kind).wait_send()
 
             @pl.when(ends[1 - d] & in_ok)
             def _(d=d):
-                from_relay(u, d).wait_send()
+                from_relay(u, d, kind).wait_send()
+
+    def first_ref(step):
+        pl.when(s != 2)(lambda: step(0))
+        pl.when(s == 2)(lambda: step(0, "left"))
+
+    def wait_sec(r):
+        sec_copy(r, 0).wait_recv()
+
+        @pl.when(s != 2)
+        def _():
+            sec_copy(r, 1).wait_recv()
 
     for d in range(2):
 
@@ -197,22 +254,18 @@
         pred_copy.wait()
         start_halo(0)
 
+    for copy in small[1:]:
+        copy.wait()
+
     def encode_row(q, f, r):
         pltpu.make_async_copy(pix_hbm.at[q, r], pix.at[q, r], pix_sem.at[q, r]).wait()
 
-        def block(b, carry):
-            x = pix[q, r, pl.ds(pl.multiple_of(b * 256, 256), 256), :]
-            hidden = jnp.maximum(
-                jnp.dot(x, w1[...], preferred_element_type=jnp.float32), 0.0
-            ).astype(jnp.bfloat16)
-            pre = jnp.dot(hidden, w2[...], preferred_element_type=jnp.float32)
-            scale = lax.rsqrt(jnp.mean(pre * pre, axis=-1, keepdims=True) + EPS)
-            f[r + 2, pl.ds(pl.multiple_of(PAD + b * 256, 16), 256), :] = (
-                pre * scale * gain[...]
-            ).astype(jnp.bfloat16)
-            return carry
-
-        lax.fori_loop(0, COLS // 256, block, 0)
+        hidden = jnp.maximum(
+            jnp.dot(pix[q, r], w1[...], preferred_element_type=jnp.float32), 0.0
+        ).astype(jnp.bfloat16)
+        pre = jnp.dot(hidden, w2[...], preferred_element_type=jnp.float32)
+        scale = lax.rsqrt(jnp.mean(pre * pre, axis=-1, keepdims=True) + EPS)
+        f[r + 2, pl.ds(PAD, COLS), :] = (pre * scale * gain[...]).astype(jnp.bfloat16)
 
     def outer_row(i):
         return jnp.where(i < 2, i, i + 4)
@@ -223,35 +276,58 @@
 
         @pl.when(s < 3)
         def _():
-            sec_copy(r).start()
+            sec_copy(r, 0).start()
+
+        @pl.when((s == 0) | (s == 2))
+        def _():
+            sec_copy(r, 1).start()
 
         return carry
 
-    lax.fori_loop(0, ROWS, encode_last, 0)
-
-    @pl.when(s == 0)
-    def _():
-        relay(0)
+    def encode_first(r):
+        encode_row(0, fa, r)
+
+        @pl.when(s == 2)
+        def _():
+            give_rows(r).start()
 
     def encode_outer(i, carry):
-        encode_row(0, fa, outer_row(i))
+        encode_first(outer_row(i))
         return carry
 
     def encode_inner(i, carry):
-        encode_row(0, fa, i + 2)
+        encode_first(i + 2)
         return carry
 
     lax.fori_loop(0, 4, encode_outer, 0)
     start_halo(1)
+
+    @pl.when(s == 2)
+    def _():
+        give_offs().start()
+
+    lax.fori_loop(0, ROWS, encode_last, 0)
+
+    @pl.when(s == 1)
+    def _():
+        start_halo(2, "right")
+
+    @pl.when(s == 0)
+    def _():
+        relay(0)
+
+    relay(1)
     lax.fori_loop(0, 4, encode_inner, 0)
 
     @pl.when(s > 0)
     def _():
         for r in (0, 1, 6, 7):
-            sec_copy(r).wait_recv()
-        start_halo(0)
-
-    relay(1)
+            wait_sec(r)
+        first_ref(start_halo)
+
+    @pl.when(s == 1)
+    def _():
+        relay(2, "right")
 
     sub = lax.broadcasted_iota(jnp.int32, (8, 128), 0)
     lane = lax.broadcasted_iota(jnp.int32, (8, 128), 1)
@@ -264,12 +340,18 @@
             picked = jnp.where(which == k, g[8 * k : 8 * k + 8], picked)
         return picked
 
-    def score_block(q, own, ref, pair, c):
+    def score_block(own, own_r, own_c, ref, offs_at, flow_at, given, pair, c):
         c0 = pl.multiple_of(c * 128, 128)
         r0 = pair * 2
-        rhs = own[pl.ds(r0 + 2, 2), pl.ds(pl.multiple_of(c0 + PAD, 16), 128), :].reshape(256, 128)
+        rhs = own[
+            pl.ds(r0 + own_r, 2), pl.ds(pl.multiple_of(c0 + own_c, 16), 128), :
+        ].reshape(256, 128)
         bands = ([], [])
+        ends_given = {0: 0, 3: 5} if given else {}
         for k in range(6):
+            if ends_given.get(pair) == k:
+                bands[k // 5].append(brecv[k // 5, :, pl.ds(c0, 128)].astype(jnp.float32))
+                continue
             lhs = ref[r0 + k, pl.ds(c0, 160), :]
             g = lax.dot_general(
                 lhs, rhs, (((1,), (1,)), ((), ())), preferred_element_type=jnp.float32
@@ -279,8 +361,8 @@
                     bands[j].append(diagonals(g[:, 128 * j : 128 * j + 128]))
         for j in range(2):
             r = r0 + j
-            oy = jnp.broadcast_to(offs[q, 0, pl.ds(r, 1), pl.ds(c0, 128)], (8, 128))
-            ox = jnp.broadcast_to(offs[q, 1, pl.ds(r, 1), pl.ds(c0, 128)], (8, 128))
+            oy = jnp.broadcast_to(offs_at(0, r, c0)[...], (8, 128))
+            ox = jnp.broadcast_to(offs_at(1, r, c0)[...], (8, 128))
             spin = turn + ox + 1
             band = bands[j]
             for bit in (1, 2, 4):
@@ -299,17 +381,70 @@
             sum_x = every2 - every
             flow_y = oy.astype(jnp.float32) + sum_y / total
             flow_x = ox.astype(jnp.float32) + sum_x / total
-            flow[q, 0, pl.ds(REACH + r, 1), pl.ds(c0, 128)] = flow_y[0:1]
-            flow[q, 1, pl.ds(REACH + r, 1), pl.ds(c0, 128)] = flow_x[0:1]
-
-    def score_pairs(q, own, ref, pairs):
+            flow_at(0, r, c0)[...] = flow_y[0:1]
+            flow_at(1, r, c0)[...] = flow_x[0:1]
+
+    def score_pairs(pairs, blocks, *where):
         for pair in pairs:
 
             def one(c, carry, pair=pair):
-                score_block(q, own, ref, pair, c)
+                score_block(*where, pair, c)
                 return carry
 
-            lax.fori_loop(0, COLS // 128, one, 0)
+            lax.fori_loop(*blocks, one, 0, unroll=blocks[1] - blocks[0])
+
+    def offs_of(q):
+        return lambda comp, r, c0: offs.at[q, comp, pl.ds(r, 1), pl.ds(c0, 128)]
+
+    def flow_of(q):
+        return lambda comp, r, c0: flow.at[q, comp, pl.ds(REACH + r, 1), pl.ds(c0, 128)]
+
+    def score_second(pairs):
+        score_pairs(pairs, (0, 8), fb, 2, PAD, fa, offs_of(1), flow_of(1), False)
+
+    def score_first(pairs):
+        part = (fa, 2, PAD, fp, offs_of(0), flow_of(0), True)
+        score_pairs(pairs, (0, 4), *part)
+
+        @pl.when(s != 2)
+        def _():
+            score_pairs(pairs, (4, 8), *part)
+
+    def score_given():
+        score_pairs(
+            (0, 1, 2, 3), (4, 8), ga, 0, -HALF, fb,
+            lambda comp, r, c0: goffs.at[comp, pl.ds(r, 1), pl.ds(c0 - HALF, 128)],
+            lambda comp, r, c0: gflow.at[comp, pl.ds(r, 1), pl.ds(c0 - HALF, 128)],
+            False,
+        )
+
+    def score_bands():
+        def one(c, carry):
+            c0 = pl.multiple_of(c * 128, 128)
+            for d in range(2):
+                lhs = fp[8 if d == 0 else 3, pl.ds(c0, 160), :]
+                rhs = fa[10 if d == 0 else 1, pl.ds(pl.multiple_of(c0 + PAD, 16), 128), :]
+                g = lax.dot_general(
+                    lhs, rhs, (((1,), (1,)), ((), ())), preferred_element_type=jnp.float32
+                )
+                bsend[d, :, pl.ds(c0, 128)] = diagonals(g).astype(jnp.bfloat16)
+            return carry
+
+        lax.fori_loop(0, 4, one, 0, unroll=4)
+
+        @pl.when(s == 2)
+        def _():
+            bsend[:, :, pl.ds(HALF, HALF)] = jnp.zeros((2, 8, HALF), jnp.bfloat16)
+
+        @pl.when(s != 2)
+        def _():
+            lax.fori_loop(4, 8, one, 0, unroll=4)
+
+        for d in range(2):
+
+            @pl.when(has[d])
+            def _(d=d):
+                band_copy(d).start()
 
     def send_flow(q):
         fsend[q] = jnp.concatenate(
@@ -321,20 +456,46 @@
             def _(d=d):
                 flow_copy(q, d).start()
 
-    score_pairs(1, fb, fa, (1, 2))
+    score_second((1, 2))
 
     @pl.when(s > 0)
     def _():
-        relay(0)
+        first_ref(relay)
+
+    wait_halo(1)
+    score_bands()
+    score_second((0, 3))
+    send_flow(1)
+
+    @pl.when(s > 0)
+    def _():
         for r in (2, 3, 4, 5):
-            sec_copy(r).wait_recv()
-
-    score_pairs(0, fa, fp, (1, 2))
-    wait_halo(1)
-    score_pairs(1, fb, fa, (0, 3))
-    send_flow(1)
-    wait_halo(0)
-    score_pairs(0, fa, fp, (0, 3))
+            wait_sec(r)
+
+    score_first((1, 2))
+
+    @pl.when(s == 1)
+    def _():
+        wait_halo(2, "right")
+        give_offs().wait_recv()
+        for r in range(ROWS):
+            give_rows(r).wait_recv()
+        score_given()
+        give_flow().start()
+
+    first_ref(wait_halo)
+    for d in range(2):
+
+        @pl.when(has[1 - d])
+        def _(d=d):
+            band_copy(d).wait_recv()
+
+    score_first((0, 3))
+
+    @pl.when(s == 2)
+    def _():
+        give_flow().wait_recv()
+
     send_flow(0)
 
     for d in range(2):
@@ -421,16 +582,33 @@
         @pl.when(has[d])
         def _(d=d):
             mask_copy(d).wait_send()
+            band_copy(d).wait_send()
             for q in range(2):
                 flow_copy(q, d).wait_send()
 
-    for u in range(2):
-        drain_halo(u)
+    drain_halo(1)
+    first_ref(drain_halo)
+
+    @pl.when(s == 1)
+    def _():
+        drain_halo(2, "right")
+        give_flow().wait_send()
+
+    @pl.when(s == 2)
+    def _():
+        give_offs().wait_send()
+        for r in range(ROWS):
+            give_rows(r).wait_send()
 
     @pl.when(s < 3)
     def _():
         for r in range(ROWS):
-            sec_copy(r).wait_send()
+            sec_copy(r, 0).wait_send()
+
+    @pl.when((s == 0) | (s == 2))
+    def _():
+        for r in range(ROWS):
+            sec_copy(r, 1).wait_send()
 
     for k in (1, 2, 3):
 
@@ -441,20 +619,30 @@
 
 def shards(pixels, pred_features, offsets, valid_mask, base_shift, w_hidden, w_feature, feat_gain):
     vm = pl.BlockSpec(memory_space=pltpu.VMEM)
-    hbm = pl.BlockSpec(memory_space=pl.ANY)
+    hbm = pl.BlockSpec(memory_space=pltpu.HBM)
     dma = pltpu.SemaphoreType.DMA
     bf = jnp.bfloat16
     summed = pl.pallas_call(
         body,
         out_shape=jax.ShapeDtypeStruct((2, 2, ROWS, COLS), jnp.float32),
-        in_specs=[hbm, hbm, vm, vm, vm, vm, vm],
+        in_specs=[hbm] * 7,
         out_specs=vm,
         scratch_shapes=[
+            pltpu.VMEM((2, 2, ROWS, COLS), jnp.int32),
+            pltpu.VMEM((2, ROWS, COLS), jnp.int32),
+            pltpu.VMEM((256, 512), bf),
+            pltpu.VMEM((512, 128), bf),
+            pltpu.VMEM((1, 128), jnp.float32),
             pltpu.VMEM((2, ROWS, COLS, 256), bf),
             pltpu.VMEM((ROWS + 4, WIDE, 128), bf),
             pltpu.VMEM((ROWS + 4, WIDE, 128), bf),
             pltpu.VMEM((ROWS + 4, WIDE, 128), bf),
-            pltpu.VMEM((2, 2, HALF, 128), bf),
+            pltpu.VMEM((ROWS, HALF, 128), bf),
+            pltpu.VMEM((2, ROWS, HALF), jnp.int32),
+            pltpu.VMEM((2, ROWS, HALF), jnp.float32),
+            pltpu.VMEM((2, 8, COLS), bf),
+            pltpu.VMEM((2, 8, COLS), bf),
+            pltpu.VMEM((3, 2, HALF, 128), bf),
             pltpu.VMEM((16, COLS), bf),
             pltpu.VMEM((2, 16, COLS), bf),
             pltpu.VMEM((2, 2, ALL, COLS), jnp.float32),
@@ -462,23 +650,30 @@
             pltpu.VMEM((2, 2, 16, COLS), bf),
             pltpu.VMEM((16, COLS), bf),
             pltpu.VMEM((3, 16, COLS), bf),
+            dma((5,)),
             dma((2, ROWS)),
             dma,
-            dma((ROWS,)),
-            dma((ROWS,)),
-            dma((2, 2, 2)),
-            dma((2, 2, 2)),
-            dma((2,)),
-            dma((2,)),
+            dma((ROWS, 2)),
+            dma((ROWS, 2)),
+            dma((3, 2, 2)),
+            dma((3, 2, 2)),
+            dma((3,)),
+            dma((3,)),
             dma((2,)),
             dma((2,)),
             dma((2, 2)),
             dma((2, 2)),
             dma((3,)),
             dma((3,)),
+            dma((ROWS,)),
+            dma((ROWS,)),
+            dma((2,)),
+            dma((2,)),
+            dma((2,)),
+            dma((2,)),
         ],
         compiler_params=pltpu.CompilerParams(
-            collective_id=0, has_side_effects=True, vmem_limit_bytes=48 << 20
+            collective_id=0, has_side_effects=True, vmem_limit_bytes=60 << 20
         ),
         name="align",
     )(

time: 84.6 us -> 63.1 us (0.75)
  Pallas kernels: 77.8 us -> 61.4 us
  local copies, waits for them, and re-layouts: 5.84 us -> 0.01 us
  other arithmetic: 0.67 us -> 1.57 us
    pallas_call x1, Pallas kernels: 77.8 us -> 61.4 us  [shards(): pl.pallas_call(body, out_shape=jax.ShapeDtypeStruct((2, 2, ROWS, COLS), j...]
    unnamed x14 -> x2, local copies, waits for them, and re-layouts: 5.84 us -> 0.01 us
    add x1, other arithmetic: 0.67 us -> 1.57 us  [shards(): return summed + base_shift[None]]
where the time goes in v2:
time: 63.1 us; the launch traced here: 63 us
  Pallas kernels  61.4 us (97%)
  other arithmetic  1.57 us (2%)
    pallas_call x1, Pallas kernels, shards(): pl.pallas_call(body, out_shape=jax.ShapeDtypeStruct((2, 2, ROWS, COLS), j...  61.4 us
    add x1, other arithmetic, shards(): return summed + base_shift[None]  1.57 us

profile of v2, /device:TPU:39, one launch (start us, length us, event | category | flops | bytes accessed | tf_op | source)
XLA Modules:
  0.0 63.0 jit_solution(3502965397040455654)
XLA Ops:
  0.0 0.0 copy-start
  0.0 61.4 %align.1 = f32[2,2,8,1024]{3,2,1,0:T(8,128)} custom-call(bf16[2,8,1024,256]{3,2,1,0:T(8,128)(2,1)} %pix_hbm.1, bf16[8,1024,128]{2,1,0:T(8,128)(2,1)} %pred_hbm.1, s32[2,2,8,1024]{3,2,1,0:T(8,128)} %offs_hbm.1, s32[2,8,1024]{2,1,0:T(8,128)} %mask_hbm.1, bf16[256,512]{1,0:T(8,128)(2,1)} %w1_hbm.1, bf16[512,128]{1,0:T(8,128)(2,1)} %w2_hbm.1, f32[1,128]{1,0:T(1,128)} %bitcast.1), custom_call_target="tpu_custom_call" | custom-call | tf_op jit(solution)/shard_map/align/pallas_call | solution.py:625
  61.4 0.0 copy-done
  61.5 1.6 %broadcast_add_fusion = f32[2,2,8,1024]{3,2,1,0:T(8,128)} fusion(f32[2,2,8,1024]{3,2,1,0:T(8,128)} %align.1, f32[2,8,1024]{2,1,0:T(8,128)S(1)} %copy-done), kind=kLoop, calls=%fused_computation | loop fusion | flops 32768 | bytes 327680 | tf_op jit(solution)/shard_map/add | solution.py:682
Async XLA Ops:
  0.0 61.4 %copy-start = (f32[2,8,1024]{2,1,0:T(8,128)S(1)}, f32[2,8,1024]{2,1,0:T(8,128)}, u32[]{:S(2)}) copy-start(f32[2,8,1024]{2,1,0:T(8,128)} %param.12) | copy-start | bytes 196612

commit v3 on v2

--- a/solution.py
+++ b/solution.py
@@ -75,33 +75,6 @@
     def _():
         pred_copy.start()
 
-    zero_side = jnp.zeros((ROWS + 4, PAD, 128), jnp.bfloat16)
-    for f in (fp, fa, fb):
-        f[:, pl.ds(0, PAD), :] = zero_side
-        f[:, pl.ds(PAD + COLS, PAD), :] = zero_side
-    zero_rows = jnp.zeros((2, COLS, 128), jnp.bfloat16)
-
-    @pl.when(jnp.logical_not(has_u))
-    def _():
-        for f in (fp, fa, fb):
-            f[pl.ds(0, 2), pl.ds(PAD, COLS), :] = zero_rows
-        mrecv[0] = jnp.zeros((16, COLS), jnp.bfloat16)
-        brecv[0] = jnp.zeros((8, COLS), jnp.bfloat16)
-        for q in range(2):
-            frecv[q, 0] = jnp.zeros((16, COLS), jnp.bfloat16)
-
-    @pl.when(jnp.logical_not(has_d))
-    def _():
-        for f in (fp, fa, fb):
-            f[pl.ds(ROWS + 2, 2), pl.ds(PAD, COLS), :] = zero_rows
-        mrecv[1] = jnp.zeros((16, COLS), jnp.bfloat16)
-        brecv[1] = jnp.zeros((8, COLS), jnp.bfloat16)
-        for q in range(2):
-            frecv[q, 1] = jnp.zeros((16, COLS), jnp.bfloat16)
-
-    small[0].wait()
-    msend[...] = jnp.concatenate([mask[0], mask[1]], axis=0).astype(jnp.float32).astype(jnp.bfloat16)
-
     barrier = pltpu.get_barrier_semaphore()
     count = jnp.int32(0)
     for ok, device in (
@@ -121,7 +94,33 @@
         pl.semaphore_signal(
             barrier, inc=1, device_id=(t, lax.rem(s + k, 4)), device_id_type=MESH
         )
-    pl.semaphore_wait(barrier, count + 3)
+
+    zero_side = jnp.zeros((ROWS + 4, PAD, 128), jnp.bfloat16)
+    for f in (fp, fa, fb):
+        f[:, pl.ds(0, PAD), :] = zero_side
+        f[:, pl.ds(PAD + COLS, PAD), :] = zero_side
+    zero_rows = jnp.zeros((2, COLS, 128), jnp.bfloat16)
+
+    @pl.when(jnp.logical_not(has_u))
+    def _():
+        for f in (fp, fa, fb):
+            f[pl.ds(0, 2), pl.ds(PAD, COLS), :] = zero_rows
+        mrecv[0] = jnp.zeros((16, COLS), jnp.bfloat16)
+        brecv[0] = jnp.zeros((8, COLS), jnp.bfloat16)
+        for q in range(2):
+            frecv[q, 0] = jnp.zeros((16, COLS), jnp.bfloat16)
+
+    @pl.when(jnp.logical_not(has_d))
+    def _():
+        for f in (fp, fa, fb):
+            f[pl.ds(ROWS + 2, 2), pl.ds(PAD, COLS), :] = zero_rows
+        mrecv[1] = jnp.zeros((16, COLS), jnp.bfloat16)
+        brecv[1] = jnp.zeros((8, COLS), jnp.bfloat16)
+        for q in range(2):
+            frecv[q, 1] = jnp.zeros((16, COLS), jnp.bfloat16)
+
+    small[0].wait()
+    msend[...] = jnp.concatenate([mask[0], mask[1]], axis=0).astype(jnp.float32).astype(jnp.bfloat16)
 
     def mask_copy(d):
         return remote(msend, mrecv.at[d], m_s.at[d], m_r.at[d], ((td, tu)[d], s))
@@ -155,11 +154,15 @@
 
     deep = (1, 2, 2)
 
-    def halo_src(u, d, span):
-        return feats[u].at[pl.ds(ROWS + 2 - deep[u] if d == 0 else 2, deep[u]), pl.ds(*span)]
-
-    def halo_dst(u, d, span):
-        return feats[u].at[pl.ds(2 - deep[u] if d == 0 else ROWS + 2, deep[u]), pl.ds(*span)]
+    def halo_src(u, d, span, row=None):
+        start = ROWS + 2 - deep[u] if d == 0 else 2
+        rows = pl.ds(start, deep[u]) if row is None else pl.ds(start + row, 1)
+        return feats[u].at[rows, pl.ds(*span)]
+
+    def halo_dst(u, d, span, row=None):
+        start = 2 - deep[u] if d == 0 else ROWS + 2
+        rows = pl.ds(start, deep[u]) if row is None else pl.ds(start + row, 1)
+        return feats[u].at[rows, pl.ds(*span)]
 
     def direct(u, d, h, kind):
         span = SPANS[kind][h]
@@ -168,18 +171,18 @@
             ((td, tu)[d], s),
         )
 
-    def to_relay(u, d, kind):
+    def to_relay(u, d, kind, row):
         span = SPANS[kind][1]
         return remote(
-            halo_src(u, d, span), rel.at[u, pl.ds(0, deep[u]), pl.ds(0, span[1])], halo_s.at[u, d, 1], rel_r.at[u],
-            (rel_dev, s),
-        )
-
-    def from_relay(u, d, kind):
+            halo_src(u, d, span, row), rel.at[u, pl.ds(row, 1), pl.ds(0, span[1])],
+            halo_s.at[u, d, 1], rel_r.at[u, row], (rel_dev, s),
+        )
+
+    def from_relay(u, d, kind, row):
         span = SPANS[kind][1]
         return remote(
-            rel.at[u, pl.ds(0, deep[u]), pl.ds(0, span[1])], halo_dst(u, d, span), rel_s.at[u], halo_r.at[u, d, 1],
-            (rel_dst, s),
+            rel.at[u, pl.ds(row, 1), pl.ds(0, span[1])], halo_dst(u, d, span, row),
+            rel_s.at[u, row], halo_r.at[u, d, 1], (rel_dst, s),
         )
 
     ends = (high, low)
@@ -191,7 +194,8 @@
 
             @pl.when(edge)
             def _(d=d):
-                to_relay(u, d, kind).start()
+                for row in range(deep[u]):
+                    to_relay(u, d, kind, row).start()
 
         for d in range(2):
             edge = ends[d] & has[d]
@@ -204,13 +208,14 @@
             def _(d=d):
                 direct(u, d, 1, kind).start()
 
-    def relay(u, kind="full"):
+    def relay(u, kind="full", rows=None):
         for d in range(2):
 
             @pl.when(ends[1 - d] & in_ok)
             def _(d=d):
-                to_relay(u, d, kind).wait_recv()
-                from_relay(u, d, kind).start()
+                for row in rows or range(deep[u]):
+                    to_relay(u, d, kind, row).wait_recv()
+                    from_relay(u, d, kind, row).start()
 
     def wait_halo(u, kind="full"):
         for d in range(2):
@@ -230,7 +235,8 @@
 
             @pl.when(ends[1 - d] & in_ok)
             def _(d=d):
-                from_relay(u, d, kind).wait_send()
+                for row in range(deep[u]):
+                    from_relay(u, d, kind, row).wait_send()
 
     def first_ref(step):
         pl.when(s != 2)(lambda: step(0))
@@ -243,23 +249,24 @@
         def _():
             sec_copy(r, 1).wait_recv()
 
+    pl.semaphore_wait(barrier, count + 3)
+
+    @pl.when(s == 0)
+    def _():
+        pred_copy.wait()
+        start_halo(0)
+
     for d in range(2):
 
         @pl.when(has[d])
         def _(d=d):
             mask_copy(d).start()
 
-    @pl.when(s == 0)
-    def _():
-        pred_copy.wait()
-        start_halo(0)
-
     for copy in small[1:]:
         copy.wait()
 
     def encode_row(q, f, r):
         pltpu.make_async_copy(pix_hbm.at[q, r], pix.at[q, r], pix_sem.at[q, r]).wait()
-
         hidden = jnp.maximum(
             jnp.dot(pix[q, r], w1[...], preferred_element_type=jnp.float32), 0.0
         ).astype(jnp.bfloat16)
@@ -270,10 +277,12 @@
     def outer_row(i):
         return jnp.where(i < 2, i, i + 4)
 
-    def encode_last(i, carry):
-        r = jnp.where(i < 4, outer_row(i), i - 2)
-        encode_row(1, fb, r)
-
+    def encode_outer(i, carry):
+        encode_row(0, fa, outer_row(i))
+        return carry
+
+    lax.fori_loop(0, 4, encode_outer, 0)
+    def send_last(r):
         @pl.when(s < 3)
         def _():
             sec_copy(r, 0).start()
@@ -282,31 +291,34 @@
         def _():
             sec_copy(r, 1).start()
 
+    start_halo(1)
+
+    @pl.when(s == 2)
+    def _():
+        give_offs().start()
+        for r in (0, 1, 6, 7):
+            give_rows(r).start()
+
+    def encode_last_outer(i, carry):
+        encode_row(1, fb, outer_row(i))
+        send_last(outer_row(i))
         return carry
 
-    def encode_first(r):
-        encode_row(0, fa, r)
+    def encode_last_inner(i, carry):
+        encode_row(1, fb, i + 2)
+        send_last(i + 2)
+        return carry
+
+    def encode_inner(i, carry):
+        encode_row(0, fa, i + 2)
 
         @pl.when(s == 2)
         def _():
-            give_rows(r).start()
-
-    def encode_outer(i, carry):
-        encode_first(outer_row(i))
+            give_rows(i + 2).start()
+
         return carry
 
-    def encode_inner(i, carry):
-        encode_first(i + 2)
-        return carry
-
-    lax.fori_loop(0, 4, encode_outer, 0)
-    start_halo(1)
-
-    @pl.when(s == 2)
-    def _():
-        give_offs().start()
-
-    lax.fori_loop(0, ROWS, encode_last, 0)
+    lax.fori_loop(0, 4, encode_last_outer, 0)
 
     @pl.when(s == 1)
     def _():
@@ -316,14 +328,24 @@
     def _():
         relay(0)
 
-    relay(1)
-    lax.fori_loop(0, 4, encode_inner, 0)
-
-    @pl.when(s > 0)
+    lax.fori_loop(0, 2, encode_last_inner, 0)
+    relay(1, rows=(0,))
+    lax.fori_loop(2, 4, encode_last_inner, 0)
+    relay(1, rows=(1,))
+
+    @pl.when((s == 1) | (s == 3))
     def _():
         for r in (0, 1, 6, 7):
             wait_sec(r)
-        first_ref(start_halo)
+        start_halo(0)
+
+    lax.fori_loop(0, 4, encode_inner, 0)
+
+    @pl.when(s == 2)
+    def _():
+        for r in (0, 1, 6, 7):
+            wait_sec(r)
+        start_halo(0, "left")
 
     @pl.when(s == 1)
     def _():
@@ -657,8 +679,8 @@
             dma((ROWS, 2)),
             dma((3, 2, 2)),
             dma((3, 2, 2)),
-            dma((3,)),
-            dma((3,)),
+            dma((3, 2)),
+            dma((3, 2)),
             dma((2,)),
             dma((2,)),
             dma((2, 2)),

time: 63.1 us -> 59.8 us (0.948)
  Pallas kernels: 61.4 us -> 58.1 us
    pallas_call x1, Pallas kernels: 61.4 us -> 58.1 us  [shards(): pl.pallas_call(body, out_shape=jax.ShapeDtypeStruct((2, 2, ROWS, COLS), j...]
where the time goes in v3:
time: 59.8 us; the launch traced here: 59.7 us
  Pallas kernels  58.1 us (97%)
  other arithmetic  1.57 us (3%)
    pallas_call x1, Pallas kernels, shards(): pl.pallas_call(body, out_shape=jax.ShapeDtypeStruct((2, 2, ROWS, COLS), j...  58.1 us
    add x1, other arithmetic, shards(): return summed + base_shift[None]  1.57 us

profile of v3, /device:TPU:39, one launch (start us, length us, event | category | flops | bytes accessed | tf_op | source)
XLA Modules:
  0.0 59.7 jit_solution(10365934250472289449)
XLA Ops:
  0.0 0.0 copy-start
  0.0 58.1 %align.1 = f32[2,2,8,1024]{3,2,1,0:T(8,128)} custom-call(bf16[2,8,1024,256]{3,2,1,0:T(8,128)(2,1)} %pix_hbm.1, bf16[8,1024,128]{2,1,0:T(8,128)(2,1)} %pred_hbm.1, s32[2,2,8,1024]{3,2,1,0:T(8,128)} %offs_hbm.1, s32[2,8,1024]{2,1,0:T(8,128)} %mask_hbm.1, bf16[256,512]{1,0:T(8,128)(2,1)} %w1_hbm.1, bf16[512,128]{1,0:T(8,128)(2,1)} %w2_hbm.1, f32[1,128]{1,0:T(1,128)} %bitcast.1), custom_call_target="tpu_custom_call" | custom-call | tf_op jit(solution)/shard_map/align/pallas_call | solution.py:647
  58.1 0.0 copy-done
  58.2 1.6 %broadcast_add_fusion = f32[2,2,8,1024]{3,2,1,0:T(8,128)} fusion(f32[2,2,8,1024]{3,2,1,0:T(8,128)} %align.1, f32[2,8,1024]{2,1,0:T(8,128)S(1)} %copy-done), kind=kLoop, calls=%fused_computation | loop fusion | flops 32768 | bytes 327680 | tf_op jit(solution)/shard_map/add | solution.py:704
Async XLA Ops:
  0.0 58.1 %copy-start = (f32[2,8,1024]{2,1,0:T(8,128)S(1)}, f32[2,8,1024]{2,1,0:T(8,128)}, u32[]{:S(2)}) copy-start(f32[2,8,1024]{2,1,0:T(8,128)} %param.12) | copy-start | bytes 196612
